TPU v7x, 32 devices: a whole 2x2x4 slice. The times are simulated.
32 devices in a mesh: groups: 2 (over y), dp: 16 (over z, x, core).
Axes of the slice: x: 2, y: 2, z: 4, core: 2. Of those that a mesh axis runs over, the one named last changes fastest.
Arguments:
- query_acts: bfloat16 [4096, 8192], P(('groups', 'dp')), parts along dimension 0, may hold values from -6 to 6
- cotangent: bfloat16 [4096, 8192], P(('groups', 'dp')), parts along dimension 0, may hold values from -6 to 6
- conv_weight: float32 [4, 4, 8192], replicated, may hold values from -3 to 3
- conv_bias: float32 [4, 8192], replicated, may hold values from -3 to 3
- owner_map: int32 [4], replicated, may hold values from 0 to 15, as said below
- basis_store: float32 [16, 25, 8192], P('dp'), may hold values from -2.5 to 2.5
- lambda_store: float32 [16, 5, 8192], P('dp'), may hold values from 0.1 to 10
- train_grads: bfloat16 [256, 4, 5, 8192], P(('groups', 'dp')), parts along dimension 0, may hold values from -6 to 6
- batch_index: int32 [512], P(('groups', 'dp')), parts along dimension 0, may hold values from 0 to 127, as said below
Outputs:
- adjoint_in: bfloat16 [4096, 8192], P(('groups', 'dp')), parts along dimension 0
- scores: float32 [512], P(('groups', 'dp')), parts along dimension 0
There are 2 independent parts, one for each index of `groups`. A program takes and returns all parts, laid end to end along the dimension named above; an argument that names none is the same for every part. Nothing has to cross between parts.
Inputs may be any that keep to these rules, and one draw needn't show every extreme that they name: `owner_map`: the 4 entries are distinct. `batch_index`: entry n names a row from (n // 16) * 8 to (n // 16) * 8 + 7.
All inputs are finite; a program needn't handle non-finite values.
Results may differ from a plain program's by a relative error of at most 0.015.
Values may be sent and summed in bfloat16 or wider, within the bound.
A program may use at most 128 MiB of HBM per device.

v0:
```python
import math

import jax
import jax.numpy as jnp
from jax import lax
from jax.sharding import PartitionSpec as P


def from_behind(value, axis, steps):
    count = lax.axis_size(axis)
    first, last = (max(0, -steps), min(count, count - steps))
    return lax.ppermute(value, axis, [(source, source + steps) for source in range(first, last)])


def from_root(value, axis, source):
    kept = jnp.where(lax.axis_index(axis) == source, value, 0).astype(value.dtype)
    return lax.psum(kept, axis)


def convolve(padded, weights, bias, count):
    result = jnp.broadcast_to(bias[None, :], (count, bias.shape[0]))
    for offset in range(4):
        result = result + weights[offset][None, :] * padded[3 - offset : 3 - offset + count].astype(
            jnp.float32
        )
    return result


def silu_slope(values):
    sig = jax.nn.sigmoid(values)
    return sig * (1.0 + values * (1.0 - sig))


def scaled_apply(gradient, eigen_basis, eigen_vals, damping):
    rotated = jnp.sum(eigen_basis * gradient[:, None, :], axis=0)
    scaled = rotated / (eigen_vals + damping)
    return jnp.sum(eigen_basis * scaled[None, :, :], axis=1)


def precondition(gradient, eigen_basis, eigen_vals):
    return scaled_apply(gradient, eigen_basis, eigen_vals, 0.1 * jnp.mean(eigen_vals))


def on_device(
    query_acts,
    cotangent,
    conv_weight,
    conv_bias,
    owner_map,
    basis_store,
    lambda_store,
    train_grads,
    batch_index,
):
    tok_rows = query_acts.shape[0]
    channels = query_acts.shape[1]
    layer_count = conv_weight.shape[0]
    norm_scale = 1.0 / math.sqrt(tok_rows * lax.axis_size("dp"))
    basis_local = basis_store[0].reshape(5, 5, channels)
    vals_local = lambda_store[0]
    stream = query_acts
    saved = []
    for layer_id in range(layer_count):
        prior_rows = from_behind(stream[tok_rows - 3 :], "dp", 1)
        padded = jnp.concatenate([prior_rows, stream], axis=0)
        saved.append(padded)
        conv_out = convolve(padded, conv_weight[layer_id], conv_bias[layer_id], tok_rows)
        stream = (stream.astype(jnp.float32) + jax.nn.silu(conv_out)).astype(jnp.bfloat16)
    adjoint = cotangent
    partials = [None] * layer_count
    for layer_id in reversed(range(layer_count)):
        padded = saved[layer_id]
        conv_out = convolve(padded, conv_weight[layer_id], conv_bias[layer_id], tok_rows)
        conv_grad = (adjoint.astype(jnp.float32) * silu_slope(conv_out)).astype(jnp.bfloat16)
        next_rows = from_behind(conv_grad[:3], "dp", -1)
        grad_f = conv_grad.astype(jnp.float32)
        terms = [
            jnp.sum(padded[3 - offset : 3 - offset + tok_rows].astype(jnp.float32) * grad_f, axis=0)
            for offset in range(4)
        ]
        terms.append(jnp.sum(grad_f, axis=0))
        partial_sum = jnp.stack(terms)
        partials[layer_id] = partial_sum
        extended = jnp.concatenate([conv_grad, next_rows], axis=0)
        conv_back = jnp.zeros((tok_rows, channels), jnp.float32)
        for offset in range(4):
            conv_back = conv_back + conv_weight[layer_id, offset][None, :] * extended[
                offset : offset + tok_rows
            ].astype(jnp.float32)
        adjoint = (adjoint.astype(jnp.float32) + conv_back).astype(jnp.bfloat16)
    gradients = jnp.stack(partials)
    gradients = lax.psum(gradients, "dp")
    gradients = gradients * norm_scale
    corrected = []
    for layer_id in range(layer_count):
        eigen_basis, eigen_vals = (
            from_root(basis_local, "dp", owner_map[layer_id]),
            from_root(vals_local, "dp", owner_map[layer_id]),
        )
        corrected.append(precondition(gradients[layer_id], eigen_basis, eigen_vals))
    corrected_all = jnp.stack(corrected)
    flattened = corrected_all.reshape(-1)
    high_part = flattened.astype(jnp.bfloat16)
    low_part = (flattened - high_part.astype(jnp.float32)).astype(jnp.bfloat16)
    both_parts = jnp.stack([high_part, low_part], axis=1)
    examples = train_grads.shape[0]
    values = jnp.sum(
        jnp.dot(train_grads.reshape(examples, -1), both_parts, preferred_element_type=jnp.float32),
        axis=1,
    )
    values = values * (1.0 / math.sqrt(5 * layer_count * channels))
    local_index = batch_index - lax.axis_index("dp") * examples
    chosen = local_index[:, None] == jnp.arange(examples, dtype=jnp.int32)[None, :]
    scores = jnp.sum(jnp.where(chosen, values[None, :], 0.0), axis=1)
    return (adjoint, scores)


def solution(mesh):
    in_specs = (
        P(("groups", "dp"), None),
        P(("groups", "dp"), None),
        P(),
        P(),
        P(),
        P("dp", None, None),
        P("dp", None, None),
        P(("groups", "dp"), None, None, None),
        P(("groups", "dp")),
    )
    out_specs = (P(("groups", "dp"), None), P(("groups", "dp")))
    return jax.shard_map(
        on_device, mesh=mesh, in_specs=in_specs, out_specs=out_specs, check_vma=False
    )
```

profile of v0, /device:TPU:0, one launch (start us, length us, event | category | flops | bytes accessed | tf_op | source)
XLA Modules:
  0.0 320.8 jit_solution(1728750580678043341)
XLA Ops:
  7.2 0.9 slice.280
  8.2 2.4 collective-permute-start
  10.6 2.3 fusion.87
  12.9 1.3 fusion.88
  14.2 6.1 %fusion.22 = bf16[128,8192]{1,0:T(8,128)(2,1)S(1)} fusion(bf16[128,8192]{1,0:T(8,128)(2,1)} %param.9, bf16[3,8192]{1,0:T(4,128)(2,1)S(1)} %collective-permute-done, f32[8192]{0:T(1024)S(1)} %bitcast.79, f32[8192]{0:T(1024)S(1)} %bitcast.82, f32[8192]{0:T(1024)S(1)} %bitcast.85, f32[8192]{0:T(1024)S(1)} %bitcast.88, f32[8192]{0:T(1024)S(1)} %bitcast.123), kind=kLoop, calls=%fused_computation.73 | loop fusion | flops 28311552 | bytes 4407296 | tf_op jit(solution)/shard_map/convert_element_type | solution.py:68
  20.4 4.5 %collective-permute-start.1 = (bf16[3,8192]{1,0:T(4,128)(2,1)S(1)}, bf16[3,8192]{1,0:T(4,128)(2,1)S(1)}, u32[]{:S(2)}, u32[]{:S(2)}) collective-permute-start(bf16[3,8192]{1,0:T(4,128)(2,1)S(1)} %slice.339), channel_id=1, source_target_pairs={{0,1},{1,2},{2,3},{3,4},{4,5},{5,6},{6,7},{7,8},{8,9},{9,10},{10,1... | collective-permute-start | bytes 147464 | tf_op jit(solution)/shard_map/ppermute | solution.py:12
  24.9 0.9 collective-permute-done.1
  25.8 3.3 %fusion.24 = bf16[128,8192]{1,0:T(8,128)(2,1)S(1)} fusion(bf16[128,8192]{1,0:T(8,128)(2,1)S(1)} %fusion.22, bf16[3,8192]{1,0:T(4,128)(2,1)S(1)} %collective-permute-done.1, f32[8192]{0:T(1024)S(1)} %bitcast.91, f32[8192]{0:T(1024)S(1)} %bitcast.94, f32[8192]{0:T(1024)S(1)} %bitcast.97, f32[8192]{0:T(1024)S(1)} %bitcast.100, f32[8192]{0:T(1024)S(1)} %bitcast.125), kind=kLoop, calls=%fused_computation.75 | loop fusion | flops 28311552 | bytes 4407296 | tf_op jit(solution)/shard_map/convert_element_type | solution.py:68
  29.1 1.3 copy-done
  30.4 2.5 collective-permute-start.2
  36.2 6.0 %fusion.26 = bf16[128,8192]{1,0:T(8,128)(2,1)S(1)} fusion(bf16[128,8192]{1,0:T(8,128)(2,1)} %copy-done, bf16[3,8192]{1,0:T(4,128)(2,1)S(1)} %collective-permute-done.2, f32[8192]{0:T(1024)S(1)} %bitcast.103, f32[8192]{0:T(1024)S(1)} %bitcast.106, f32[8192]{0:T(1024)S(1)} %bitcast.109, f32[8192]{0:T(1024)S(1)} %bitcast.112, f32[8192]{0:T(1024)S(1)} %bitcast.127), kind=kLoop, calls=%fused_computation.77 | loop fusion | flops 28311552 | bytes 4407296 | tf_op jit(solution)/shard_map/convert_element_type | solution.py:68
  42.3 4.3 %collective-permute-start.3 = (bf16[3,8192]{1,0:T(4,128)(2,1)S(1)}, bf16[3,8192]{1,0:T(4,128)(2,1)S(1)}, u32[]{:S(2)}, u32[]{:S(2)}) collective-permute-start(bf16[3,8192]{1,0:T(4,128)(2,1)S(1)} %slice.349), channel_id=1, source_target_pairs={{0,1},{1,2},{2,3},{3,4},{4,5},{5,6},{6,7},{7,8},{8,9},{9,10},{10,1... | collective-permute-start | bytes 147464 | tf_op jit(solution)/shard_map/ppermute | solution.py:12
  47.4 6.8 %fusion.33 = (f32[8192]{0:T(1024)S(1)}, f32[8192]{0:T(1024)}, f32[8192]{0:T(1024)}, f32[8192]{0:T(1024)}, f32[8192]{0:T(1024)}, /*index=5*/bf16[128,8192]{1,0:T(8,128)(2,1)S(1)}) fusion(bf16[128,8192]{1,0:T(8,128)(2,1)S(1)} %fusion.26, bf16[3,8192]{1,0:T(4,128)(2,1)S(1)} %collective-permute-done.3, f32[8192]{0:T(1024)S(1)} %bitcast.119, ...), kind=kLoop, calls=%fused_computation.84 | loop fusion | flops 51339264 | bytes 6668288 | tf_op jit(solution)/shard_map/reduce_sum | solution.py:78
  54.2 1.3 collective-permute-start.4
  55.5 1.0 copy_bitcast_fusion
  56.5 1.2 collective-permute-done.4
  57.7 9.3 %fusion.40 = (f32[8192]{0:T(1024)}, f32[8192]{0:T(1024)}, f32[8192]{0:T(1024)}, f32[8192]{0:T(1024)}, f32[8192]{0:T(1024)}, /*index=5*/bf16[128,8192]{1,0:T(8,128)(2,1)S(1)}, bf16[128,8192]{1,0:T(8,128)(2,1)S(1)}) fusion(bf16[128,8192]{1,0:T(8,128)(2,1)S(1)} %copy-done.1, bf16[3,8192]{1,0:T(4,128)(2,1)S(1)} %collective-permute-done.2, ...), kind=kLoop, calls=%fused_computation.91 | loop fusion | flops 75456512 | bytes 11042816 | tf_op jit(solution)/shard_map/reduce_sum | solution.py:78
  67.1 1.3 collective-permute-start.5
  68.4 1.0 copy_bitcast_fusion.2
  69.3 4.2 %collective-permute-done.5 = bf16[3,8192]{1,0:T(4,128)(2,1)S(1)} collective-permute-done((bf16[3,8192]{1,0:T(4,128)(2,1)S(1)}, bf16[3,8192]{1,0:T(4,128)(2,1)S(1)}, u32[]{:S(2)}, u32[]{:S(2)}) %collective-permute-start.5) | collective-permute-done | bytes 49184 | tf_op jit(solution)/shard_map/ppermute | solution.py:12
  73.5 10.0 %fusion.47 = (f32[8192]{0:T(1024)}, f32[8192]{0:T(1024)}, f32[8192]{0:T(1024)}, f32[8192]{0:T(1024)}, f32[8192]{0:T(1024)}, /*index=5*/bf16[128,8192]{1,0:T(8,128)(2,1)S(1)}, bf16[128,8192]{1,0:T(8,128)(2,1)}) fusion(bf16[128,8192]{1,0:T(8,128)(2,1)S(1)} %fusion.22, bf16[3,8192]{1,0:T(4,128)(2,1)S(1)} %collective-permute-done.1, f32[8192]{0:T(1024)S(1)} %bitcast.92, ...), kind=kLoop, calls=%fused_computation.98 | loop fusion | flops 75456512 | bytes 11042816 | tf_op jit(solution)/shard_map/reduce_sum | solution.py:78
  83.5 1.3 copy-done.2
  85.5 1.5 collective-permute-start.6
  86.9 9.4 %fusion.71 = (f32[25,8192]{1,0:T(8,128)S(1)}, f32[25,8192]{1,0:T(8,128)S(1)}, f32[25,8192]{1,0:T(8,128)}, f32[25,8192]{1,0:T(8,128)S(1)}) fusion(f32[1,25,8192]{2,0,1:T(1,128)S(1)} %copy-done.15, pred[]{:T(512)S(6)} %eq.32, pred[]{:T(512)S(6)} %eq.33, pred[]{:T(512)S(6)} %eq.35, pred[]{:T(512)S(6)} %eq.34), kind=kLoop, calls=%fused_computation.164 | loop fusion | flops 819200 | bytes 4096004 | tf_op jit(solution)/shard_map/jit(_where)/select_n | solution.py:16
  96.3 2.4 select_n.100
  98.8 1.2 select_n.82
  100.1 1.2 select_n.88
  101.3 1.2 select_n.94
  103.4 19.1 %fusion.54 = (f32[8192]{0:T(1024)S(1)}, f32[8192]{0:T(1024)}, f32[8192]{0:T(1024)}, f32[8192]{0:T(1024)}, f32[8192]{0:T(1024)}, /*index=5*/bf16[128,8192]{1,0:T(8,128)(2,1)S(1)}, bf16[128,8192]{1,0:T(8,128)(2,1)}) fusion(bf16[128,8192]{1,0:T(8,128)(2,1)} %param.9, bf16[3,8192]{1,0:T(4,128)(2,1)S(1)} %collective-permute-done, f32[8192]{0:T(1024)S(1)} %bitcast.80, ...), kind=kLoop, calls=%fused_computation.105 | loop fusion | flops 75456512 | bytes 11042816 | tf_op jit(solution)/shard_map/reduce_sum | solution.py:78
  122.5 1.0 stack.112
  123.5 1.1 pad_maximum_fusion.8
  124.7 1.5 collective-permute-start.7
  126.2 4.8 %copy.12 = bf16[8,4,5,8192]{3,0,2,1:T(8,128)(2,1)} copy(bf16[8,4,5,8192]{3,1,2,0:T(4,128)(2,1)} %param.16) | data formatting | bytes 5242880 | tf_op args[7]
  131.1 3.7 %fusion.20 = bf16[128,8192]{1,0:T(8,128)(2,1)} fusion(bf16[128,8192]{1,0:T(8,128)(2,1)S(1)} %copy-done.4, bf16[128,8192]{1,0:T(8,128)(2,1)S(1)} %get-tuple-element.35, bf16[3,8192]{1,0:T(4,128)(2,1)S(1)} %collective-permute-done.7, f32[8192]{0:T(1024)S(1)} %bitcast.81, f32[8192]{0:T(1024)S(1)} %bitcast.84, f32[8192]{0:T(1024)S(1)} %bitcast.87, ...), kind=kLoop, calls=%fused_computation.71 | loop fusion | flops 24117248 | bytes 6471680 | tf_op jit(solution)/shard_map/convert_element_type | solution.py:90
  134.8 154.7 %all-reduce.3.cloned.1.call-done = (f32[5,5,8192]{2,1,0:T(8,128)}, f32[4,5,8192]{2,1,0:T(8,128)}, f32[5,8192]{1,0:T(8,128)}, f32[5,5,8192]{2,1,0:T(8,128)}, f32[...) async-done(((f32[5,5,8192]{2,1,0:T(8,128)}, f32[4,5,8192]{2,1,0:T(8,128)}, f32[5,8192]{1,0:T(8,128)}, ...) | async-done | bytes 4587536 | tf_op jit(solution)/shard_map/psum | solution.py:17
  289.4 1.5 broadcast_multiply_fusion
  290.9 1.0 slice_bitcast_fusion.3
  293.4 1.0 add_divide_fusion.6
  294.3 1.1 multiply_reduce_fusion.6
  296.8 1.1 multiply_reduce_fusion.5
  298.0 1.1 multiply_reduce_fusion.4
  299.1 1.7 reduce_sum.333
  301.5 1.1 multiply_reduce_fusion.3
  302.7 1.0 add_divide_fusion.4
  303.7 1.1 multiply_reduce_fusion.2
  306.2 1.1 multiply_reduce_fusion.1
  307.9 0.8 reshape.123
  309.5 3.9 %convolution_reduce_fusion = f32[8]{0:T(128)S(1)} fusion(bf16[8,163840]{1,0:T(8,128)(2,1)} %bitcast.70, bf16[163840,1]{0,1:T(2,128)(2,1)S(1)} %get-tuple-element.47, bf16[163840,1]{0,1:T(2,128)(2,1)S(1)} %get-tuple-element.46), kind=kOutput, calls=%fused_computation.161 | convolution fusion | flops 6553608 | bytes 3276832 | tf_op jit(solution)/shard_map/dot_general | solution.py:108
  (95 shorter events, 7.4 us)
Async XLA Ops:
  7.2 282.3 %all-reduce.3.cloned.1.call-start = ((), (), s32[]{:S(2)}) async-start(), calls=%async_computation | async-start | bytes 14680064 | tf_op jit(solution)/shard_map/psum | solution.py:17
  8.2 6.0 %collective-permute-start = (bf16[3,8192]{1,0:T(4,128)(2,1)S(1)}, bf16[3,8192]{1,0:T(4,128)(2,1)S(1)}, u32[]{:S(2)}, u32[]{:S(2)}) collective-permute-start(bf16[3,8192]{1,0:T(4,128)(2,1)S(1)} %slice.280), channel_id=1, source_target_pairs={{0,1},{1,2},{2,3},{3,4},{4,5},{5,6},{6,7},{7,8},{8,9},{9,10},{10,1... | collective-permute-start | bytes 147464 | tf_op jit(solution)/shard_map/ppermute | solution.py:12
  20.3 12.7 %copy-start.31 = (s32[4]{0:T(128)S(1)}, s32[4]{0:T(128)}, u32[]{:S(2)}) copy-start(s32[4]{0:T(128)} %param.13) | copy-start | bytes 52
  20.4 5.4 %collective-permute-start.1 = (bf16[3,8192]{1,0:T(4,128)(2,1)S(1)}, bf16[3,8192]{1,0:T(4,128)(2,1)S(1)}, u32[]{:S(2)}, u32[]{:S(2)}) collective-permute-start(bf16[3,8192]{1,0:T(4,128)(2,1)S(1)} %slice.339), channel_id=1, source_target_pairs={{0,1},{1,2},{2,3},{3,4},{4,5},{5,6},{6,7},{7,8},{8,9},{9,10},{10,1... | collective-permute-start | bytes 147464 | tf_op jit(solution)/shard_map/ppermute | solution.py:12
  29.1 1.3 copy-start
  30.4 16.1 %copy-start.16 = (f32[1,5,8192]{2,0,1:T(1,128)S(1)}, f32[1,5,8192]{2,0,1:T(1,128)}, u32[]{:S(2)}) copy-start(f32[1,5,8192]{2,0,1:T(1,128)} %param.15) | copy-start | bytes 491524
  30.4 5.8 %collective-permute-start.2 = (bf16[3,8192]{1,0:T(4,128)(2,1)S(1)}, bf16[3,8192]{1,0:T(4,128)(2,1)S(1)}, u32[]{:S(2)}, u32[]{:S(2)}) collective-permute-start(bf16[3,8192]{1,0:T(4,128)(2,1)S(1)} %slice.344), channel_id=1, source_target_pairs={{0,1},{1,2},{2,3},{3,4},{4,5},{5,6},{6,7},{7,8},{8,9},{9,10},{10,1... | collective-permute-start | bytes 147464 | tf_op jit(solution)/shard_map/ppermute | solution.py:12
  36.2 11.2 %copy-start.3 = (bf16[128,8192]{1,0:T(8,128)(2,1)S(1)}, bf16[128,8192]{1,0:T(8,128)(2,1)}, u32[]{:S(2)}) copy-start(bf16[128,8192]{1,0:T(8,128)(2,1)} %param.10) | copy-start | bytes 6291460
  42.3 5.2 %collective-permute-start.3 = (bf16[3,8192]{1,0:T(4,128)(2,1)S(1)}, bf16[3,8192]{1,0:T(4,128)(2,1)S(1)}, u32[]{:S(2)}, u32[]{:S(2)}) collective-permute-start(bf16[3,8192]{1,0:T(4,128)(2,1)S(1)} %slice.349), channel_id=1, source_target_pairs={{0,1},{1,2},{2,3},{3,4},{4,5},{5,6},{6,7},{7,8},{8,9},{9,10},{10,1... | collective-permute-start | bytes 147464 | tf_op jit(solution)/shard_map/ppermute | solution.py:12
  47.4 10.3 %copy-start.1 = (bf16[128,8192]{1,0:T(8,128)(2,1)S(1)}, bf16[128,8192]{1,0:T(8,128)(2,1)}, u32[]{:S(2)}) copy-start(bf16[128,8192]{1,0:T(8,128)(2,1)} %copy-done) | copy-start | bytes 6291460
  54.2 3.5 %collective-permute-start.4 = (bf16[3,8192]{1,0:T(4,128)(2,1)S(1)}, bf16[3,8192]{1,0:T(4,128)(2,1)S(1)}, u32[]{:S(2)}, u32[]{:S(2)}) collective-permute-start(bf16[3,8192]{1,0:T(4,128)(2,1)S(1)} %slice.354), channel_id=1, source_target_pairs={{1,0},{2,1},{3,2},{4,3},{5,4},{6,5},{7,6},{8,7},{9,8},{10,9},{11,1... | collective-permute-start | bytes 147464 | tf_op jit(solution)/shard_map/ppermute | solution.py:12
  67.1 6.5 %collective-permute-start.5 = (bf16[3,8192]{1,0:T(4,128)(2,1)S(1)}, bf16[3,8192]{1,0:T(4,128)(2,1)S(1)}, u32[]{:S(2)}, u32[]{:S(2)}) collective-permute-start(bf16[3,8192]{1,0:T(4,128)(2,1)S(1)} %slice.359), channel_id=1, source_target_pairs={{1,0},{2,1},{3,2},{4,3},{5,4},{6,5},{7,6},{8,7},{9,8},{10,9},{11,1... | collective-permute-start | bytes 147464 | tf_op jit(solution)/shard_map/ppermute | solution.py:12
  73.5 13.4 %copy-start.15 = (f32[1,25,8192]{2,0,1:T(1,128)S(1)}, f32[1,25,8192]{2,0,1:T(1,128)}, u32[]{:S(2)}) copy-start(f32[1,25,8192]{2,0,1:T(1,128)} %param.14) | copy-start | bytes 2457604
  83.5 1.4 copy-start.2
  85.5 17.9 %collective-permute-start.6 = (bf16[3,8192]{1,0:T(4,128)(2,1)}, bf16[3,8192]{1,0:T(4,128)(2,1)}, u32[]{:S(2)}, u32[]{:S(2)}) collective-permute-start(bf16[3,8192]{1,0:T(4,128)(2,1)} %slice.364), channel_id=1, source_target_pairs={{1,0},{2,1},{3,2},{4,3},{5,4},{6,5},{7,6},{8,7},{9,8},{10,9},{11,1... | collective-permute-start | bytes 147464 | tf_op jit(solution)/shard_map/ppermute | solution.py:12
  99.9 2.6 copy-start.17
  99.9 2.6 copy-start.18
  99.9 2.6 copy-start.19
  100.0 2.6 copy-start.20
  100.0 2.8 copy-start.21
  100.0 2.8 copy-start.22
  100.0 2.8 copy-start.23
  100.0 2.8 copy-start.24
  100.0 2.8 copy-start.25
  100.0 3.1 copy-start.26
  100.0 3.1 copy-start.27
  100.0 3.1 copy-start.28
  100.0 3.1 copy-start.29
  100.0 3.1 copy-start.30
  124.6 1.6 copy-start.32
  124.7 6.4 %collective-permute-start.7 = (bf16[3,8192]{1,0:T(4,128)(2,1)S(1)}, bf16[3,8192]{1,0:T(4,128)(2,1)S(1)}, u32[]{:S(2)}, u32[]{:S(2)}) collective-permute-start(bf16[3,8192]{1,0:T(4,128)(2,1)S(1)} %slice.369), channel_id=1, source_target_pairs={{1,0},{2,1},{3,2},{4,3},{5,4},{6,5},{7,6},{8,7},{9,8},{10,9},{11,1... | collective-permute-start | bytes 147464 | tf_op jit(solution)/shard_map/ppermute | solution.py:12
  126.2 4.9 %copy-start.4 = (bf16[128,8192]{1,0:T(8,128)(2,1)S(1)}, bf16[128,8192]{1,0:T(8,128)(2,1)}, u32[]{:S(2)}) copy-start(bf16[128,8192]{1,0:T(8,128)(2,1)} %get-tuple-element.36) | copy-start | bytes 6291460
  289.4 2.4 copy-start.8
  289.4 2.6 copy-start.11
  291.9 3.6 %copy-start.10 = (f32[5,8192]{1,0:T(8,128)S(1)}, f32[5,8192]{1,0:T(8,128)}, u32[]{:S(2)}) copy-start(f32[5,8192]{1,0:T(8,128)} %get-tuple-element.32) | copy-start | bytes 491524
  291.9 4.9 %copy-start.7 = (f32[5,5,8192]{2,1,0:T(8,128)S(1)}, f32[5,5,8192]{2,1,0:T(8,128)}, u32[]{:S(2)}) copy-start(f32[5,5,8192]{2,1,0:T(8,128)} %get-tuple-element.31) | copy-start | bytes 2457604
  295.5 6.1 %copy-start.6 = (f32[5,5,8192]{2,1,0:T(8,128)S(1)}, f32[5,5,8192]{2,1,0:T(8,128)}, u32[]{:S(2)}) copy-start(f32[5,5,8192]{2,1,0:T(8,128)} %get-tuple-element.29) | copy-start | bytes 2457604
  299.1 5.7 %copy-start.9 = (f32[5,8192]{1,0:T(8,128)S(1)}, f32[5,8192]{1,0:T(8,128)}, u32[]{:S(2)}) copy-start(f32[5,8192]{1,0:T(8,128)} %get-tuple-element.28) | copy-start | bytes 491524
  299.1 7.0 %copy-start.5 = (f32[5,5,8192]{2,1,0:T(8,128)S(1)}, f32[5,5,8192]{2,1,0:T(8,128)}, u32[]{:S(2)}) copy-start(f32[5,5,8192]{2,1,0:T(8,128)} %get-tuple-element.26) | copy-start | bytes 2457604
  304.8 3.0 copy-start.12
  304.8 3.0 copy-start.13
  304.8 3.0 copy-start.14
Sparse Core Ops, SparseCore 0:
  124.7 164.6 all-reduce.2
where the time goes:
time: 322 us; the launch traced here: 321 us
  waiting for transfers between devices  161 us (50%)
  other arithmetic  91.5 us (28%)
  local copies, waits for them, and re-layouts  25.2 us (8%)
  between operations  19.8 us (6%)
  starting transfers between devices  19.3 us (6%)
  matrix products  3.89 us (1%)
    psum x1, waiting for transfers between devices, from_root(): return lax.psum(kept, axis)  155 us
    reduce_sum x4, other arithmetic, on_device(): jnp.sum(padded[3 - offset:3 - offset + tok_rows].astype(jnp.float32) * gr...  45.2 us
    ppermute x8, starting transfers between devices, from_behind(): lax.ppermute(value, axis, [(source, source + steps) for source in range(f...  19.2 us
    convert_element_type x3, other arithmetic, on_device(): (stream.astype(jnp.float32) + jax.nn.silu(conv_out)).astype(jnp.bfloat16)  15.4 us
    select_n x2, other arithmetic, from_root(): jnp.where(lax.axis_index(axis) == source, value, 0).astype(value.dtype)  10 us
    unnamed x69, local copies, waits for them, and re-layouts  9.62 us
    ppermute x8, waiting for transfers between devices, from_behind(): lax.ppermute(value, axis, [(source, source + steps) for source in range(f...  6.49 us
  transfers between devices with their start and end apart: 9, of which 5 were waited for; matrix products, arithmetic and copies ran while one was open for 10% of the time, Pallas kernels for 0%

commit v1 on v0

v1 whole, which is shorter than its diff:
```python
import functools
import math

import jax
import jax.numpy as jnp
import numpy as np
from jax import lax
from jax.experimental import pallas as pl
from jax.experimental.pallas import tpu as pltpu
from jax.sharding import PartitionSpec as P

LANES = 128
SUB = 8
TAPS = 4
HALO_ROWS = 16
PAIRS = [(j, k) for j in range(5) for k in range(j, 5)]


def layout_plan(rows, layers):
    reach = (TAPS - 1) * layers
    extended = rows + 2 * reach
    fold = -(-extended // SUB)
    padded = -(-(fold * SUB) // 16) * 16
    return reach, fold, padded


def permutations(rows, layers):
    reach, fold, padded = layout_plan(rows, layers)
    columns = rows + 2 * HALO_ROWS
    into = np.zeros((padded, columns), np.float32)
    back = np.zeros((rows, padded), np.float32)
    for j in range(fold):
        for s in range(SUB):
            token = fold * s + j - reach
            row = SUB * j + s
            if 0 <= token < rows:
                into[row, token] = 1.0
                back[token, row] = 1.0
            elif -reach <= token < 0:
                into[row, rows + HALO_ROWS + token] = 1.0
            elif rows <= token < rows + reach:
                into[row, HALO_ROWS + token] = 1.0
    return jnp.asarray(into, jnp.bfloat16), jnp.asarray(back, jnp.bfloat16)


def rounded(value):
    return value.astype(jnp.bfloat16).astype(jnp.float32)


def window_chunk(lanes, rows, layers, is_first, w_ref, b_ref, x_all, c_all, slope_all, g_ref):
    reach, fold, padded = layout_plan(rows, layers)
    sub = lax.broadcasted_iota(jnp.int32, (SUB, LANES), 0)
    edges = {}

    def own(j, low, high):
        tokens = [fold * s + j - reach for s in range(SUB)]
        inside = tuple(low <= t < high for t in tokens)
        if all(inside):
            return None
        if inside not in edges:
            lead = next(i for i, ok in enumerate(inside) if ok)
            tail = max(i for i, ok in enumerate(inside) if ok)
            edges[inside] = (sub >= lead) & (sub <= tail)
        return edges[inside]

    zero = jnp.zeros((SUB, LANES), jnp.float32)

    def keep(value, mask):
        return value if mask is None else jnp.where(mask, value, zero)

    def row(ref, *at):
        return jnp.broadcast_to(ref[at[:-1] + (pl.ds(at[-1], 1), lanes)], (SUB, LANES))

    live = {}

    def begun(j):
        mask = own(j, 0, 1 << 30)
        if mask is None:
            return None
        key = id(mask)
        if key not in live:
            live[key] = mask | jnp.logical_not(is_first)
        return live[key]

    last = TAPS - 1
    for layer in range(layers):
        taps = [row(w_ref, layer, k) * 0.5 for k in range(TAPS)]
        bias = row(b_ref, layer) * 0.5
        base = layer * (fold + last) * SUB
        for i in range(last):
            wrapped = x_all[pl.ds(base + (fold + i) * SUB, SUB), lanes]
            x_all[pl.ds(base + i * SUB, SUB), lanes] = pltpu.roll(wrapped, 1, 0)
        x = [x_all[pl.ds(base + i * SUB, SUB), lanes] for i in range(fold + last)]
        following = base + (fold + last + last) * SUB
        for j in range(fold):
            half = bias
            for k in range(TAPS):
                half = half + taps[k] * x[last + j - k]
            bent = jnp.tanh(half)
            up = 1.0 + bent
            slope_all[pl.ds((layer * fold + j) * SUB, SUB), lanes] = up * (1.0 + half * (1.0 - bent))
            if layer < layers - 1:
                fresh = keep(rounded(x[last + j] + half * up), begun(j))
                x_all[pl.ds(following + j * SUB, SUB), lanes] = fresh
    for layer in reversed(range(layers)):
        taps = [row(w_ref, layer, k) * 0.5 for k in range(TAPS)]
        base = layer * (fold + last) * SUB
        doubled = [None] * (fold + last)
        sums = [zero] * (TAPS + 1)

        def at(i):
            return x_all[pl.ds(base + i * SUB, SUB), lanes]

        for j in range(fold):
            adjoint = c_all[pl.ds(j * SUB, SUB), lanes]
            slope = slope_all[pl.ds((layer * fold + j) * SUB, SUB), lanes]
            grad = keep(rounded(adjoint * slope), own(j, 0, 1 << 30))
            doubled[j] = grad
            if j < last:
                doubled[fold + j] = pltpu.roll(grad, SUB - 1, 0)
            inner = keep(grad, own(j, -(1 << 30), rows))
            for k in range(TAPS):
                sums[k] = sums[k] + at(last + j - k) * inner
            sums[TAPS] = sums[TAPS] + inner
        for j in range(fold):
            total = c_all[pl.ds(j * SUB, SUB), lanes]
            back = taps[0] * doubled[j]
            for k in range(1, TAPS):
                back = back + taps[k] * doubled[j + k]
            c_all[pl.ds(j * SUB, SUB), lanes] = rounded(total + back)
        for k in range(TAPS + 1):
            g_ref[pl.ds(layer * 5 + k, 1), lanes] = 0.5 * jnp.sum(sums[k], axis=0, keepdims=True)


def window_kernel(rows, layers, x_ref, c_ref, hx_ref, hc_ref, w_ref, b_ref, into_ref, back_ref,
                  out_ref, g_ref, x_all, c_all, slope_all):
    reach, fold, padded = layout_plan(rows, layers)
    width = x_ref.shape[1]
    is_first = lax.axis_index("dp") == 0
    count = fold * SUB
    acts = jnp.concatenate([x_ref[...], hx_ref[...]], axis=0)
    cots = jnp.concatenate([c_ref[...], hc_ref[...]], axis=0)
    x_all[pl.ds((TAPS - 1) * SUB, count), :] = jnp.dot(
        into_ref[...], acts, preferred_element_type=jnp.float32)[:count]
    c_all[...] = jnp.dot(into_ref[...], cots, preferred_element_type=jnp.float32)

    @pl.loop(0, width // LANES)
    def _(chunk):
        lanes = pl.ds(pl.multiple_of(chunk * LANES, LANES), LANES)
        window_chunk(lanes, rows, layers, is_first, w_ref, b_ref, x_all, c_all, slope_all, g_ref)

    out_ref[...] = jnp.dot(
        back_ref[...], c_all[...].astype(jnp.bfloat16), preferred_element_type=jnp.float32
    ).astype(jnp.bfloat16)


def window(acts, cots, halo_acts, halo_cots, weights, bias):
    rows, channels = acts.shape
    layers = weights.shape[0]
    reach, fold, padded = layout_plan(rows, layers)
    width = 512
    into, back = permutations(rows, layers)
    block = lambda *lead: pl.BlockSpec(lead + (width,), lambda i: (0,) * len(lead) + (i,))
    whole = lambda a: pl.BlockSpec(a.shape, lambda i: (0, 0))
    return pl.pallas_call(
        functools.partial(window_kernel, rows, layers),
        grid=(channels // width,),
        out_shape=(
            jax.ShapeDtypeStruct((rows, channels), jnp.bfloat16),
            jax.ShapeDtypeStruct((layers * 5, channels), jnp.float32),
        ),
        in_specs=[
            block(rows), block(rows), block(2 * HALO_ROWS), block(2 * HALO_ROWS),
            block(layers, TAPS), block(layers), whole(into), whole(back),
        ],
        out_specs=(block(rows), block(layers * 5)),
        scratch_shapes=[
            pltpu.VMEM((layers * (fold + TAPS - 1) * SUB, width), jnp.float32),
            pltpu.VMEM((padded, width), jnp.float32),
            pltpu.VMEM((layers * fold * SUB, width), jnp.float32),
        ],
        compiler_params=pltpu.CompilerParams(vmem_limit_bytes=24 << 20),
        cost_estimate=pl.CostEstimate(flops=200_000_000, bytes_accessed=10_000_000, transcendentals=5_000_000),
    )(acts, cots, halo_acts, halo_cots, weights, bias, into, back)


def shifted(value, axis, steps):
    count = lax.axis_size(axis)
    first, final = (max(0, -steps), min(count, count - steps))
    return lax.ppermute(value, axis, [(s, s + steps) for s in range(first, final)])


def inverse_rows(basis, vals):
    channels = basis.shape[-1]
    blocks = basis.reshape(5, 5, channels)
    scale = 1.0 / (vals + 0.1 * jnp.mean(vals))
    return jnp.stack([jnp.sum(blocks[j] * blocks[k] * scale, axis=0) for j, k in PAIRS])


def on_device(query_acts, cotangent, conv_weight, conv_bias, owner_map, basis_store, lambda_store,
              train_grads, batch_index):
    rows, channels = query_acts.shape
    layers = conv_weight.shape[0]
    here = lax.axis_index("dp")
    norm_scale = 1.0 / math.sqrt(rows * lax.axis_size("dp"))
    before = shifted(query_acts[rows - HALO_ROWS:], "dp", 1)
    after = shifted(jnp.concatenate([query_acts[:HALO_ROWS], cotangent[:HALO_ROWS]]), "dp", -1)
    halo_acts = jnp.concatenate([before, after[:HALO_ROWS]])
    halo_cots = jnp.concatenate([jnp.zeros_like(before), after[HALO_ROWS:]])
    own_rows = inverse_rows(basis_store[0], lambda_store[0])
    held = jnp.where((owner_map == here)[:, None, None], own_rows[None], 0.0)
    inverse = lax.psum_scatter(held, "dp", scatter_dimension=2, tiled=True)
    adjoint, partial = window(query_acts, cotangent, halo_acts, halo_cots, conv_weight, conv_bias)
    summed = lax.psum_scatter(partial, "dp", scatter_dimension=1, tiled=True) * norm_scale
    summed = summed.reshape(layers, 5, -1)
    order = {pair: i for i, pair in enumerate(PAIRS)}
    corrected = jnp.stack([
        sum(inverse[:, order[min(j, k), max(j, k)]] * summed[:, k] for k in range(5))
        for j in range(5)
    ], axis=1)
    everyone = lax.all_gather(corrected, "dp", axis=2, tiled=True)
    high = everyone.astype(jnp.bfloat16)
    low = (everyone - high.astype(jnp.float32)).astype(jnp.bfloat16)
    both = high.astype(jnp.float32) + low.astype(jnp.float32)
    examples = train_grads.shape[0]
    values = jnp.sum(train_grads.astype(jnp.float32) * both[None], axis=(1, 2, 3))
    values = values * (1.0 / math.sqrt(5 * layers * channels))
    local_index = batch_index - here * examples
    chosen = local_index[:, None] == jnp.arange(examples, dtype=jnp.int32)[None, :]
    scores = jnp.sum(jnp.where(chosen, values[None, :], 0.0), axis=1)
    return (adjoint, scores)


def solution(mesh):
    in_specs = (
        P(("groups", "dp"), None),
        P(("groups", "dp"), None),
        P(),
        P(),
        P(),
        P("dp", None, None),
        P("dp", None, None),
        P(("groups", "dp"), None, None, None),
        P(("groups", "dp")),
    )
    out_specs = (P(("groups", "dp"), None), P(("groups", "dp")))
    return jax.shard_map(
        on_device, mesh=mesh, in_specs=in_specs, out_specs=out_specs, check_vma=False
    )
```

time: 322 us -> 280 us (0.87)
  waiting for transfers between devices: 161 us -> 74 us
  local copies, waits for them, and re-layouts: 25.2 us -> 112 us
  other arithmetic: 91.5 us -> 14.3 us
  Pallas kernels: 0 us -> 37.5 us
  blocking collectives: 0 us -> 20.7 us
  starting transfers between devices: 19.3 us -> 5.11 us
  between operations: 19.8 us -> 14.9 us
  matrix products: 3.89 us -> 0 us
    psum x1 -> x0, waiting for transfers between devices: 155 us -> none  [from_root(): return lax.psum(kept, axis)]
    unnamed x69 -> x40, local copies, waits for them, and re-layouts: 9.62 us -> 91.3 us
    unnamed x1 -> x3, waiting for transfers between devices: 0.02 us -> 74 us
    reduce_sum x16 -> x4, other arithmetic: 56.3 us -> 8.98 us  [the longest x2 6.52 us: inverse_rows(): jnp.sum(blocks[j] * blocks[k] * scale, axis=0)]
    pallas_call x0 -> x1, Pallas kernels: none -> 37.5 us  [window(): pl.pallas_call(functools.partial(window_kernel, rows, layers), grid=(chan...]
    all_gather x0 -> x1, blocking collectives: none -> 20.7 us  [on_device(): everyone = lax.all_gather(corrected, 'dp', axis=2, tiled=True)]
    convert_element_type x5 -> x0, other arithmetic: 19.9 us -> none  [the longest x3 15.4 us: on_device(): (stream.astype(jnp.float32) + jax.nn.silu(conv_out)).astype(jnp.bfloat16)]
    ppermute x8 -> x2, starting transfers between devices: 19.2 us -> 5.03 us  [shifted(): lax.ppermute(value, axis, [(s, s + steps) for s in range(first, final)])]
  transfers between devices with their start and end apart: 9 -> 4, of which waited for: 5 -> 1; matrix products, arithmetic and copies ran while one was open for 10% -> 33% of each run, Pallas kernels for 0% -> 0%
where the time goes in v1:
time: 280 us; the launch traced here: 279 us
  local copies, waits for them, and re-layouts  112 us (40%)
  waiting for transfers between devices  74 us (26%)
  Pallas kernels  37.5 us (13%)
  blocking collectives  20.7 us (7%)
  between operations  14.9 us (5%)
  other arithmetic  14.3 us (5%)
  starting transfers between devices  5.11 us (2%)
    unnamed x40, local copies, waits for them, and re-layouts  91.3 us
    unnamed x3, waiting for transfers between devices  74 us
    pallas_call x1, Pallas kernels, window(): pl.pallas_call(functools.partial(window_kernel, rows, layers), grid=(chan...  37.5 us
    all_gather x1, blocking collectives, on_device(): everyone = lax.all_gather(corrected, 'dp', axis=2, tiled=True)  20.7 us
    slice x1, local copies, waits for them, and re-layouts, on_device(): inverse[:, order[min(j, k), max(j, k)]] * summed[:, k]  14.4 us
    reduce_sum x2, other arithmetic, inverse_rows(): jnp.sum(blocks[j] * blocks[k] * scale, axis=0)  6.52 us
  transfers between devices with their start and end apart: 4, of which 1 were waited for; matrix products, arithmetic and copies ran while one was open for 33% of the time, Pallas kernels for 0%

profile of v1, /device:TPU:0, one launch (start us, length us, event | category | flops | bytes accessed | tf_op | source)
XLA Modules:
  0.0 278.5 jit_solution(506445222025945731)
XLA Ops:
  7.2 0.0 copy-start.6
  7.2 0.0 reduce-scatter.5.cloned.1.call-start
  7.2 1.8 fusion.2
  9.1 1.0 slice.67
  10.0 0.8 pad_maximum_fusion
  10.9 1.3 collective-permute-start.1
  12.2 3.8 %collective-permute-start = (bf16[16,8192]{1,0:T(8,128)(2,1)}, bf16[16,8192]{1,0:T(8,128)(2,1)}, u32[]{:S(2)}, u32[]{:S(2)}) collective-permute-start(bf16[16,8192]{1,0:T(8,128)(2,1)} %get-tuple-element.37), channel_id=1, source_target_pairs={{0,1},{1,2},{2,3},{3,4},{4,5},{5,6},{6,7},{7,8},{8,9},{9,10},{10,1... | collective-permute-start | bytes 786440 | tf_op jit(solution)/shard_map/ppermute | solution.py:190
  15.9 0.9 reduce_sum.162
  17.5 0.0 copy-start.4
  17.5 3.6 %multiply_reduce_fusion.1 = (f32[8192]{0:T(1024)S(1)}, f32[8192]{0:T(1024)S(1)}, f32[8192]{0:T(1024)S(1)}, f32[8192]{0:T(1024)S(1)}, f32[8192]{0:T(1024)}, /*ind...) fusion(f32[1,25,8192]{2,0,1:T(1,128)S(1)} %copy-done.6, ...), kind=kLoop, calls=%fused_computation.7 | loop fusion | flops 1343488 | bytes 1507332 | tf_op jit(solution)/shard_map/reduce_sum | solution.py:197
  21.2 2.9 %multiply_reduce_fusion.12 = (f32[8192]{0:T(1024)}, f32[8192]{0:T(1024)}, f32[8192]{0:T(1024)}, f32[8192]{0:T(1024)}) fusion(f32[1,5,8192]{2,0,1:T(1,128)S(1)} %get-tuple-element.21, f32[1,25,8192]{2,0,1:T(1,128)} %param.16), kind=kLoop, calls=%fused_computation.18 | loop fusion | flops 458752 | bytes 950272 | tf_op jit(solution)/shard_map/reduce_sum | solution.py:197
  24.1 2.4 stack.71
  26.4 0.0 copy-start.1
  26.4 0.8 broadcast_compare_fusion
  27.2 1.1 fusion.3
  28.4 1.0 pad_maximum_fusion.1.hx_ref
  29.4 37.5 %shard_map.122 = (bf16[128,8192]{1,0:T(8,128)(2,1)}, f32[20,8192]{1,0:T(8,128)}) custom-call(bf16[128,8192]{1,0:T(8,128)(2,1)S(1)} %copy-done, bf16[128,8192]{1,0:T(8,128)(2,1)S(1)} %copy-done.1, bf16[32,8192]{1,0:T(8,128)(2,1)S(1)} %pad_maximum_fusion.1.hx_ref, bf16[32,8192]{1,0:T(8,128)(2,1)S(1)} %concatenate.11.hc_ref, f32[4,4,8192]{2,1,0:T(4,128)S(1)} %copy-done.2, ...), custom_call_target="tpu_custom_call" | custom-call | flops 200000000 | bytes 10000000 | tf_op jit(solution)/shard_map/pallas_call | solution.py:165
  66.9 0.0 reduce-scatter.5.cloned.1.call-update
  66.9 0.0 reduce-scatter.7.cloned.1.call-start
  67.0 0.6 broadcast_select_fusion
  67.5 32.6 %copy.26 = f32[4,15,8192]{0,1,2:T(8,128)} copy(f32[4,15,8192]{2,0,1:T(4,128)S(1)} %broadcast_select_fusion) | data formatting | bytes 3932160
  100.1 45.2 %reshape.59 = f32[8192,60]{1,0:T(8,128)} reshape(f32[8192,15,4]{2,1,0:T(8,128)} %bitcast.1) | data formatting | bytes 3932160
  145.4 0.0 reduce-scatter.7.cloned.1.call-update
  145.4 0.6 copy-done.9
  146.0 0.5 broadcast_subtract_fusion
  146.5 0.8 broadcast_multiply_fusion
  147.4 73.9 %reduce-scatter.7.cloned.1.call-done = f32[512,60]{1,0:T(8,128)} async-done(((f32[8192,60]{1,0:T(8,128)}), f32[512,60]{1,0:T(8,128)}) %reduce-scatter.7.cloned.1.call-update) | async-done | bytes 122896
  221.3 4.3 %reshape.60 = f32[512,15,4]{2,1,0:T(8,128)} reshape(f32[512,60]{1,0:T(8,128)} %reduce-scatter.7.cloned.1.call-done) | data formatting | bytes 245760
  225.6 14.4 %fusion.1 = (f32[4,1,512]{0,1,2:T(1,128)S(1)}, f32[4,1,512]{0,1,2:T(1,128)S(1)}, f32[4,1,512]{0,1,2:T(1,128)S(1)}, f32[4,1,512]{0,1,2:T(1,128)}, f32[4,1,512]{0,...) fusion(f32[4,15,512]{0,1,2:T(8,128)} %bitcast.18), kind=kLoop, calls=%fused_computation.34 | loop fusion | bytes 245760 | tf_op jit(solution)/shard_map/slice | solution.py:218
  240.0 0.1 copy.28
  240.1 0.1 copy.30
  240.2 0.1 copy.32
  240.3 0.1 copy.34
  240.5 0.1 copy.36
  240.6 1.2 copy.38
  241.8 1.1 copy.39
  242.9 1.1 copy.40
  244.0 1.1 copy.41
  245.0 1.1 copy.42
  246.1 1.1 copy.43
  247.2 1.1 copy.44
  248.2 0.1 copy.45
  248.3 0.1 copy.46
  248.5 0.1 copy.47
  248.7 20.7 %all_gather.3 = f32[4,5,8192]{2,0,1:T(4,128)S(1)} all-gather(f32[4,5,512]{2,0,1:T(4,128)S(1)} %constant_dynamic-update-slice_fusion), channel_id=1, replica_groups=mesh['groups'=2,'dp'=16] {'dp'}, dimensions={2}, use_global_device_ids=true | all-gather | bytes 696320 | tf_op jit(solution)/shard_map/all_gather | solution.py:221
  269.4 0.1 convert_add_fusion
  269.6 1.5 multiply_reduce_fusion
  271.1 0.6 select_reduce_fusion
  (30 shorter events, 0.3 us)
Async XLA Ops:
  7.2 8.8 %copy-start.8 = (f32[1,5,8192]{2,0,1:T(1,128)S(1)}, f32[1,5,8192]{2,0,1:T(1,128)}, u32[]{:S(2)}) copy-start(f32[1,5,8192]{2,0,1:T(1,128)} %param.17) | copy-start | bytes 491524
  7.2 10.3 %copy-start.6 = (f32[1,25,8192]{2,0,1:T(1,128)S(1)}, f32[1,25,8192]{2,0,1:T(1,128)}, u32[]{:S(2)}) copy-start(f32[1,25,8192]{2,0,1:T(1,128)} %param.16) | copy-start | bytes 2457604
  7.2 139.4 %reduce-scatter.5.cloned.1.call-start = ((), (), s32[]{:S(2)}) async-start(), calls=%async_computation.2 | async-start | bytes 835584 | tf_op jit(solution)/shard_map/reduce_scatter | solution.py:214
  10.9 16.4 %collective-permute-start.1 = (bf16[32,8192]{1,0:T(8,128)(2,1)}, bf16[32,8192]{1,0:T(8,128)(2,1)}, u32[]{:S(2)}, u32[]{:S(2)}) collective-permute-start(bf16[32,8192]{1,0:T(8,128)(2,1)} %pad_maximum_fusion), channel_id=1, source_target_pairs={{1,0},{2,1},{3,2},{4,3},{5,4},{6,5},{7,6},{8,7},{9,8},{10,9},{11,1... | collective-permute-start | bytes 1572872 | tf_op jit(solution)/shard_map/ppermute | solution.py:190
  12.2 16.2 %collective-permute-start = (bf16[16,8192]{1,0:T(8,128)(2,1)}, bf16[16,8192]{1,0:T(8,128)(2,1)}, u32[]{:S(2)}, u32[]{:S(2)}) collective-permute-start(bf16[16,8192]{1,0:T(8,128)(2,1)} %get-tuple-element.37), channel_id=1, source_target_pairs={{0,1},{1,2},{2,3},{3,4},{4,5},{5,6},{6,7},{7,8},{8,9},{9,10},{10,1... | collective-permute-start | bytes 786440 | tf_op jit(solution)/shard_map/ppermute | solution.py:190
  17.5 11.8 %copy-start.4 = (bf16[160,160]{1,0:T(8,128)(2,1)S(1)}, bf16[160,160]{1,0:T(8,128)(2,1)}, u32[]{:S(2)}) copy-start(bf16[160,160]{1,0:T(8,128)(2,1)} %constant.25.clone.into_ref) | copy-start | bytes 153604
  21.2 8.2 %copy-start = (bf16[128,8192]{1,0:T(8,128)(2,1)S(1)}, bf16[128,8192]{1,0:T(8,128)(2,1)}, u32[]{:S(2)}) copy-start(bf16[128,8192]{1,0:T(8,128)(2,1)} %x_ref.1) | copy-start | bytes 6291460
  21.2 8.2 %copy-start.2 = (f32[4,4,8192]{2,1,0:T(4,128)S(1)}, f32[4,4,8192]{2,1,0:T(4,128)}, u32[]{:S(2)}) copy-start(f32[4,4,8192]{2,1,0:T(4,128)} %w_ref.1) | copy-start | bytes 1572868
  21.2 8.2 %copy-start.3 = (f32[4,8192]{1,0:T(4,128)S(1)}, f32[4,8192]{1,0:T(4,128)}, u32[]{:S(2)}) copy-start(f32[4,8192]{1,0:T(4,128)} %b_ref.1) | copy-start | bytes 393220
  21.2 8.2 %copy-start.5 = (bf16[128,160]{1,0:T(8,128)(2,1)S(1)}, bf16[128,160]{1,0:T(8,128)(2,1)}, u32[]{:S(2)}) copy-start(bf16[128,160]{1,0:T(8,128)(2,1)} %constant.26.clone.back_ref) | copy-start | bytes 122884
  26.4 3.0 %copy-start.1 = (bf16[128,8192]{1,0:T(8,128)(2,1)S(1)}, bf16[128,8192]{1,0:T(8,128)(2,1)}, u32[]{:S(2)}) copy-start(bf16[128,8192]{1,0:T(8,128)(2,1)} %c_ref.1) | copy-start | bytes 6291460
  66.9 154.4 %reduce-scatter.7.cloned.1.call-start = ((), (), s32[]{:S(2)}) async-start(), calls=%async_computation.3 | async-start | bytes 4456448
  145.4 0.7 copy-start.9
  240.6 29.0 %copy-start.7 = (bf16[8,4,5,8192]{3,1,2,0:T(4,128)(2,1)S(1)}, bf16[8,4,5,8192]{3,1,2,0:T(4,128)(2,1)}, u32[]{:S(2)}) copy-start(bf16[8,4,5,8192]{3,1,2,0:T(4,128)(2,1)} %param.18) | copy-start | bytes 7864324
  248.7 22.4 %copy-start.10 = (s32[16]{0:T(128)S(1)}, s32[16]{0:T(128)}, u32[]{:S(2)}) copy-start(s32[16]{0:T(128)} %broadcast_subtract_fusion) | copy-start | bytes 196
Sparse Core Ops, SparseCore 0:
  67.0 59.5 reduce-scatter.4
  145.5 75.7 reduce-scatter.6
